TPU v7x, 32 devices: a whole 2x2x4 slice. The times are simulated.
32 devices in a mesh: grp: 4 (over z), pen: 8 (over y, x, core).
Axes of the slice: x: 2, y: 2, z: 4, core: 2. Of those that a mesh axis runs over, the one named last changes fastest.
Arguments:
- cell_offsets: int32 [2, 1048576], P(None, ('grp', 'pen')), may hold values from 0 to 1
- cell_z: int32 [1048576], P(('grp', 'pen')), may hold values from 0 to 255
- frac: float32 [3, 1048576], P(None, ('grp', 'pen')), may hold values from 0 to 1
- charges: float32 [1048576], P(('grp', 'pen')), may hold values from -4 to 4
- tile_counts: int32 [16384], P(('grp', 'pen')), may hold values from 16 to 64, as said below
Outputs:
- forces: float32 [3, 1048576], P(None, ('grp', 'pen'))
- energy: float32 [], replicated
Inputs may be any that keep to these rules, and one draw needn't show every extreme that they name: `tile_counts`: live slots of each tile; some tile holds 64.
All inputs are finite; a program needn't handle non-finite values.
Results may differ from a plain program's by a relative error of at most 0.0003.
Values sent between devices are 32-bit elements; how exact they have to be, the bound alone decides.
A program may use at most 256 MiB of HBM per device.

v0:
```python
import math
import jax
import jax.numpy as jnp
from jax import lax
from jax.sharding import PartitionSpec as P

KX = 256
KY = 256
KZ = 256
ATOMS = 1048576
ewald_split = 0.6
highest = lax.Precision.HIGHEST


def shifted(block, axis, distance):
    devices = range(lax.axis_size(axis))
    route = [((i - distance) % len(devices), i) for i in devices]
    return lax.ppermute(block, axis, route)


def spline_rows(fracs):
    values = [jnp.ones_like(fracs)]
    fifth = values
    for order in range(2, 7):
        nxt = []
        for j in range(order):
            term = jnp.zeros_like(fracs)
            if j >= 1:
                term = values[j - 1] * (fracs + order - 1 - j)
            if j <= order - 2:
                term = term + values[j] * (1.0 - fracs + j)
            nxt.append(term / (order - 1))
        if order == 5:
            fifth = nxt
        values = nxt
    slopes = []
    for j in range(6):
        term = jnp.zeros_like(fracs)
        if j >= 1:
            term = fifth[j - 1]
        if j <= 4:
            term = term - fifth[j]
        slopes.append(term)
    return (values, slopes)


def tile_weights(offsets, zcell, fracs, charge, counts, size_z):
    slots = charge.shape[-1]
    live = (jnp.arange(slots, dtype=jnp.int32) < counts[..., None]).astype(jnp.float32)
    live_q = charge * live
    theta_x, slope_x = spline_rows(fracs[0])
    theta_y, slope_y = spline_rows(fracs[1])
    theta_z, slope_z = spline_rows(fracs[2])
    footing = jnp.arange(8, dtype=jnp.int32)[:, None]
    cells = jnp.arange(size_z, dtype=jnp.int32)
    weight_x = 0.0
    grade_x = 0.0
    weight_y = 0.0
    grade_y = 0.0
    weight_z = 0.0
    grade_z = 0.0
    for j in range(6):
        hit_x = (footing == offsets[0][..., None, :] + j).astype(jnp.float32)
        hit_y = (footing == offsets[1][..., None, :] + j).astype(jnp.float32)
        hit_z = (cells == (zcell[..., :, None] + j) % size_z).astype(jnp.float32)
        weight_x = weight_x + theta_x[j][..., None, :] * hit_x
        grade_x = grade_x + slope_x[j][..., None, :] * hit_x
        weight_y = weight_y + theta_y[j][..., None, :] * hit_y
        grade_y = grade_y + slope_y[j][..., None, :] * hit_y
        weight_z = weight_z + theta_z[j][..., :, None] * hit_z
        grade_z = grade_z + slope_z[j][..., :, None] * hit_z
    return (weight_x, grade_x, weight_y, grade_y, weight_z, grade_z, live_q)


def modulus(index, length):
    coeffs = (1.0 / 120.0, 26.0 / 120.0, 66.0 / 120.0, 26.0 / 120.0, 1.0 / 120.0)
    real_part = 0.0
    imag_part = 0.0
    for j in range(5):
        angle = (index * j % length).astype(jnp.float32) * (2.0 * math.pi / length)
        real_part = real_part + coeffs[j] * jnp.cos(angle)
        imag_part = imag_part + coeffs[j] * jnp.sin(angle)
    return real_part * real_part + imag_part * imag_part


def influence(index_x, index_y, index_z):
    freq_x = jnp.where(2 * index_x < KX, index_x, index_x - KX).astype(jnp.float32) / KX
    freq_y = jnp.where(2 * index_y < KY, index_y, index_y - KY).astype(jnp.float32) / KY
    freq_z = jnp.where(2 * index_z < KZ, index_z, index_z - KZ).astype(jnp.float32) / KZ
    square = freq_x * freq_x + freq_y * freq_y + freq_z * freq_z
    safe = jnp.where(square > 0, square, 1.0)
    volume = float(KX * KY * KZ)
    value = jnp.exp(-math.pi**2 * safe / ewald_split**2) / (math.pi * volume * safe)
    value = value / (modulus(index_x, KX) * modulus(index_y, KY) * modulus(index_z, KZ))
    return jnp.where(square > 0, value, 0.0)


def dft_tables(length):
    index = jnp.arange(length, dtype=jnp.int32)
    angle = (index[:, None] * index[None, :] % length).astype(jnp.float32) * (
        2.0 * math.pi / length
    )
    return (jnp.cos(angle), jnp.sin(angle))


def z_slots(groups):
    planes = KZ // (2 * groups) + 1
    owner = jnp.arange(groups, dtype=jnp.int32)[:, None]
    within = jnp.arange(planes, dtype=jnp.int32)[None, :]
    ordinary = owner * (planes - 1) + within
    frequency = jnp.where(within < planes - 1, ordinary, jnp.where(owner == 0, KZ // 2, 0))
    plane_weight = jnp.where(
        within < planes - 1, jnp.where(frequency == 0, 1.0, 2.0), jnp.where(owner == 0, 1.0, 0.0)
    )
    frequency = frequency.reshape(-1)
    plane_weight = plane_weight.reshape(-1).astype(jnp.float32)
    position = jnp.arange(KZ, dtype=jnp.int32)
    angle = (frequency[:, None] * position[None, :] % KZ).astype(jnp.float32) * (2.0 * math.pi / KZ)
    usable = (plane_weight > 0).astype(jnp.float32)[:, None]
    return (planes, frequency, plane_weight, jnp.cos(angle) * usable, jnp.sin(angle) * usable)


def forward_complex(data, cos_table, sin_table, shape, axis):
    direct = jnp.dot(cos_table, data, precision=highest).reshape(shape)
    other = jnp.dot(sin_table, data, precision=highest).reshape(shape)
    real_part = jnp.take(direct, 0, axis=axis) + jnp.take(other, 1, axis=axis)
    imag_part = jnp.take(direct, 1, axis=axis) - jnp.take(other, 0, axis=axis)
    return (real_part, imag_part)


def inverse_complex(data, cos_table, sin_table, shape, axis):
    direct = jnp.dot(cos_table, data, precision=highest).reshape(shape)
    other = jnp.dot(sin_table, data, precision=highest).reshape(shape)
    real_part = jnp.take(direct, 0, axis=axis) - jnp.take(other, 1, axis=axis)
    imag_part = jnp.take(other, 0, axis=axis) + jnp.take(direct, 1, axis=axis)
    return (real_part, imag_part)


def spectrum_pen_first(grid, block_x, block_y):
    cos_x, sin_x = dft_tables(KX)
    cos_y, sin_y = dft_tables(KY)
    planes, frequency, plane_weight, cos_z, sin_z = z_slots(lax.axis_size("pen"))
    slot_total = cos_z.shape[0]
    lines = KY // lax.axis_size("grp")
    real_z = jnp.einsum("xyz,kz->ykx", grid, cos_z, precision=highest)
    imag_z = -jnp.einsum("xyz,kz->ykx", grid, sin_z, precision=highest)
    outgoing = jnp.stack([real_z, imag_z], axis=2).reshape(block_y, slot_total * 2 * block_x)
    columns = lax.all_to_all(outgoing, "pen", split_axis=1, concat_axis=0, tiled=True)
    real_y, imag_y = forward_complex(columns, cos_y, sin_y, (KY, planes, 2, block_x), 2)
    sectioned = jnp.transpose(jnp.stack([real_y, imag_y], axis=-1), (2, 0, 1, 3)).reshape(
        block_x, KY * planes * 2
    )
    rows = lax.all_to_all(sectioned, "grp", split_axis=1, concat_axis=0, tiled=True)
    real_x, imag_x = forward_complex(rows, cos_x, sin_x, (KX, lines, planes, 2), 3)
    first = lax.axis_index("pen") * planes
    index_x = jnp.arange(KX, dtype=jnp.int32)[:, None, None]
    index_y = lax.axis_index("grp") * lines + jnp.arange(lines, dtype=jnp.int32)[None, :, None]
    index_z = lax.dynamic_slice_in_dim(frequency, first, planes)[None, None, :]
    local_weight = lax.dynamic_slice_in_dim(plane_weight, first, planes)[None, None, :]
    kernel = influence(index_x, index_y, index_z)
    spectral = 0.5 * jnp.sum(local_weight * kernel * (real_x * real_x + imag_x * imag_x))
    scaled = jnp.stack([kernel * real_x, kernel * imag_x], axis=-1).reshape(KX, lines * planes * 2)
    real_b, imag_b = inverse_complex(scaled, cos_x, sin_x, (KX, lines, planes, 2), 3)
    returning = jnp.stack([real_b, imag_b], axis=-1).reshape(KX, lines * planes * 2)
    rows_home = lax.all_to_all(returning, "grp", split_axis=0, concat_axis=1, tiled=True)
    rows_home = jnp.transpose(rows_home.reshape(block_x, KY, planes, 2), (1, 2, 3, 0)).reshape(
        KY, planes * 2 * block_x
    )
    real_c, imag_c = inverse_complex(rows_home, cos_y, sin_y, (KY, planes, 2, block_x), 2)
    leaving = jnp.stack([real_c, imag_c], axis=2).reshape(KY, planes * 2 * block_x)
    home = lax.all_to_all(leaving, "pen", split_axis=0, concat_axis=1, tiled=True).reshape(
        block_y, slot_total, 2, block_x
    )
    potential = jnp.einsum(
        "ykx,kz->xyz", home[:, :, 0], plane_weight[:, None] * cos_z, precision=highest
    )
    potential = potential - jnp.einsum(
        "ykx,kz->xyz", home[:, :, 1], plane_weight[:, None] * sin_z, precision=highest
    )
    return (potential, spectral)


def place_tiles(spread, tiles_x, tiles_y):
    shaped = spread.reshape(tiles_x, tiles_y, 4, 2, 4, 2, KZ)
    total = 0.0
    for i in range(4):
        for j in range(4):
            part = jnp.transpose(shaped[:, :, i, :, j], (0, 2, 1, 3, 4)).reshape(
                2 * tiles_x, 2 * tiles_y, KZ
            )
            total = total + jnp.pad(part, ((2 * i, 6 - 2 * i), (2 * j, 6 - 2 * j), (0, 0)))
    return total


def gather_tiles(extended, tiles_x, tiles_y):
    blocks = []
    for i in range(4):
        members = []
        for j in range(4):
            part = extended[2 * i : 2 * i + 2 * tiles_x, 2 * j : 2 * j + 2 * tiles_y]
            part = part.reshape(tiles_x, 2, tiles_y, 2, KZ)
            members.append(jnp.transpose(part, (0, 2, 1, 3, 4)))
        blocks.append(jnp.stack(members, axis=3))
    return jnp.stack(blocks, axis=2).reshape(tiles_x, tiles_y, 64, KZ)


def local(cell_offsets, cell_z, frac, charges, tile_counts):
    block_x = KX // lax.axis_size("grp")
    block_y = KY // lax.axis_size("pen")
    tiles_x = block_x // 2
    tiles_y = block_y // 2
    slots = charges.shape[0] // (tiles_x * tiles_y)
    offsets = cell_offsets.reshape(2, tiles_x, tiles_y, slots)
    zcell = cell_z.reshape(tiles_x, tiles_y, slots)
    fracs = frac.reshape(3, tiles_x, tiles_y, slots)
    charge = charges.reshape(tiles_x, tiles_y, slots)
    counts = tile_counts.reshape(tiles_x, tiles_y)
    weight_x, grade_x, weight_y, grade_y, weight_z, grade_z, live_q = tile_weights(
        offsets, zcell, fracs, charge, counts, KZ
    )
    pair = weight_x[..., :, None, :] * weight_y[..., None, :, :] * live_q[..., None, None, :]
    pair = pair.reshape(tiles_x, tiles_y, 64, slots)
    spread = jnp.einsum("abfs,absz->abfz", pair, weight_z, precision=highest)
    padded = place_tiles(spread, tiles_x, tiles_y)
    rim_y = shifted(padded[: block_x + 5, block_y : block_y + 5], "pen", 1)
    merged = padded[: block_x + 5, :block_y].at[:, :5].add(rim_y)
    rim_x = shifted(merged[block_x : block_x + 5], "grp", 1)
    grid = merged[:block_x].at[:5].add(rim_x)
    potential, spectral = spectrum_pen_first(grid, block_x, block_y)
    upper = shifted(potential[:5], "grp", -1)
    ext_x = jnp.concatenate([potential, upper, jnp.zeros((1, block_y, KZ), jnp.float32)], axis=0)
    beside = shifted(ext_x[:, :5], "pen", -1)
    extended = jnp.concatenate(
        [ext_x, beside, jnp.zeros((block_x + 6, 1, KZ), jnp.float32)], axis=1
    )
    footing = gather_tiles(extended, tiles_x, tiles_y)
    main = jnp.einsum("abfz,absz->abfs", footing, weight_z, precision=highest).reshape(
        tiles_x, tiles_y, 8, 8, slots
    )
    tilt = jnp.einsum("abfz,absz->abfs", footing, grade_z, precision=highest).reshape(
        tiles_x, tiles_y, 8, 8, slots
    )
    force_x = -live_q * jnp.einsum(
        "abxs,abys,abxys->abs", grade_x, weight_y, main, precision=highest
    )
    force_y = -live_q * jnp.einsum(
        "abxs,abys,abxys->abs", weight_x, grade_y, main, precision=highest
    )
    force_z = -live_q * jnp.einsum(
        "abxs,abys,abxys->abs", weight_x, weight_y, tilt, precision=highest
    )
    total = lax.psum(spectral, ("grp", "pen"))
    forces = jnp.stack([force_x, force_y, force_z], axis=0).reshape(3, tiles_x * tiles_y * slots)
    return (forces, total / ATOMS)


def solution(mesh):
    in_specs = (
        P(None, ("grp", "pen")),
        P(("grp", "pen")),
        P(None, ("grp", "pen")),
        P(("grp", "pen")),
        P(("grp", "pen")),
    )
    out_specs = (P(None, ("grp", "pen")), P())
    return jax.shard_map(local, mesh=mesh, in_specs=in_specs, out_specs=out_specs, check_vma=False)
```

profile of v0, /device:TPU:0, one launch (start us, length us, event | category | flops | bytes accessed | tf_op | source)
XLA Modules:
  0.0 1138.8 jit_solution(11327651914012425456)
XLA Ops:
  22.6 140.7 %fusion.15 = f32[32,16,64,256]{3,2,1,0:T(8,128)} fusion(f32[32,16,64]{2,1,0:T(8,128)S(1)} %copy-done.60, s32[32,16,64]{2,1,0:T(8,128)S(1)} %get-tuple-element.184, f32[32,16,64]{2,1,0:T(8,128)S(1)} %copy-done.58, s32[32,16,64]{2,1,0:T(8,128)S(1)} %get-tuple-element.183, f32[32,16,64]{2,1,0:T(8,128)S(1)} %copy-done.54, ...), kind=kOutput, calls=%fused_computation.27 | convolution fusion | flops 6589251584 | bytes 37355520 | tf_op jit(solution)/shard_map/abfs,absz->abfz/dot_general | solution.py:223
  163.2 39.0 %reshape.1907 = f32[32,16,4,2,4,2,256]{6,5,4,3,2,1,0:T(2,128)} reshape(f32[32,16,64,256]{3,2,1,0:T(8,128)} %fusion.15) | data formatting | bytes 67108864 | tf_op jit(solution)/shard_map/reshape | solution.py:184
  202.2 25.3 %slice_bitcast_fusion.15 = (f32[32,2,16,2,256]{4,3,1,2,0:T(2,128)S(1)}, f32[32,2,16,2,256]{4,3,1,2,0:T(2,128)S(1)}, f32[32,2,16,2,256]{4,3,1,2,0:T(2,128)}, f32[...) fusion(f32[32,16,4,2,4,2,256]{6,5,4,3,2,1,0:T(2,128)} %reshape.1907), kind=kLoop, calls=%fused_computation.93 | loop fusion | bytes 67108864 | tf_op jit(solution)/shard_map/transpose | solution.py:188
  241.3 4.1 copy.276
  256.9 4.1 copy.278
  287.6 4.0 copy.282
  291.7 4.0 reshape.1916
  303.4 4.1 copy.284
  318.8 4.1 copy.286
  348.2 12.9 %pad_add_fusion = f32[70,38,256]{2,0,1:T(8,128)S(1)} fusion(f32[64,32,256]{2,0,1:T(8,128)} %reshape.1923, f32[64,32,256]{2,0,1:T(8,128)} %reshape.1922, f32[64,32,256]{2,0,1:T(8,128)} %reshape.1921, f32[64,32,256]{2,0,1:T(8,128)} %reshape.1920, f32[64,32,256]{2,0,1:T(8,128)} %reshape.1919, f32[64,32,256]{2,0,1:T(8,128)} %reshape.1918, ...), kind=kLoop, calls=%fused_computation.52 | loop fusion | flops 10214400 | bytes 36278272 | tf_op jit(solution)/shard_map/add | solution.py:191
  365.0 4.7 collective-permute-done
  375.6 5.0 collective-permute-done.1
  389.0 7.5 copy.290
  396.5 4.6 all_to_all.52
  401.6 31.4 %all_to_all.70 = f32[32,8,2176]{2,0,1:T(8,128)} all-to-all(f32[32,8,2176]{2,0,1:T(8,128)S(1)} %copy.291), channel_id=1, replica_groups=mesh['grp'=4,'pen'=8] {'pen'}, dimensions={1} | all-to-all | bytes 4456448 | tf_op jit(solution)/shard_map/all_to_all | solution.py:148
  441.5 5.1 copy.296
  446.6 5.1 copy.297
  456.4 50.4 %all-to-all-done.1 = f32[64,4,2176]{2,0,1:T(8,128)S(1)} async-done(((f32[64,4,2176]{2,0,1:T(8,128)}), f32[64,4,2176]{2,0,1:T(8,128)S(1)}, u32[]{:S(2)}, u32[]{:S(2)}) %all-to-all-start.1) | async-done | bytes 2228256 | tf_op jit(solution)/shard_map/all_to_all | solution.py:153
  535.2 4.9 all_to_all.60
  540.0 4.5 copy.311
  544.6 54.0 %all_to_all.71 = f32[4,64,2176]{2,1,0:T(8,128)} all-to-all(f32[4,64,2176]{2,1,0:T(8,128)S(1)} %copy.311), channel_id=1, replica_groups=mesh['grp'=4,'pen'=8] {'grp'}, dimensions={0} | all-to-all | bytes 4456448 | tf_op jit(solution)/shard_map/all_to_all | solution.py:165
  598.6 4.7 copy.312
  603.4 7.0 copy.372
  610.4 6.1 copy.313
  616.5 4.6 fusion.36
  624.8 5.1 copy.317
  629.9 4.6 all_to_all.63
  634.5 30.8 %all_to_all.72 = f32[8,32,2176]{2,1,0:T(8,128)S(1)} all-to-all(f32[8,32,2176]{2,1,0:T(8,128)S(1)} %all_to_all.63), channel_id=1, replica_groups=mesh['grp'=4,'pen'=8] {'pen'}, dimensions={0} | all-to-all | bytes 4456448 | tf_op jit(solution)/shard_map/all_to_all | solution.py:171
  666.6 4.1 reshape.1927
  670.7 8.8 fusion.280
  679.5 5.8 copy.378
  685.4 5.3 fusion.141
  690.6 4.5 copy.377
  695.1 4.2 fusion.143
  701.5 55.4 %select_add_fusion.1.clone.4 = f32[32,16,64,256]{3,2,1,0:T(8,128)} fusion(f32[32,16,64]{2,1,0:T(8,128)S(1)} %copy-done.61, s32[32,16,64]{2,1,0:T(8,128)S(1)} %copy-done.43, f32[32,16,64]{2,1,0:T(8,128)S(1)} %copy-done.59, s32[32,16,64]{2,1,0:T(8,128)S(1)} %copy-done.41, f32[32,16,64]{2,1,0:T(8,128)S(1)} %copy-done.55, ...), kind=kLoop, calls=%fused_computation.13.clone.clone.clone.clone.1 | loop fusion | flops 142606336 | bytes 35127296 | tf_op jit(solution)/shard_map/abxs,abys,abxys->abs/dot_general | solution.py:243
  758.3 55.3 %fusion.294 = f32[32,16,64,256]{3,2,1,0:T(8,128)} fusion(f32[32,16,64]{2,1,0:T(8,128)S(1)} %copy-done.53, f32[32,16,64]{2,1,0:T(8,128)S(1)} %copy-done.51, f32[32,16,64]{2,1,0:T(8,128)S(1)} %copy-done.50, f32[32,16,64]{2,1,0:T(8,128)S(1)} %copy-done.52, f32[32,16,64]{2,1,0:T(8,128)S(1)} %copy-done.49, f32[32,16,64]{2,1,0:T(8,128)S(1)} %copy-done.48, ...), kind=kLoop, calls=%fused_computation.2.clone.clone.clone.1 | loop fusion | flops 142606336 | bytes 35127296 | tf_op jit(solution)/shard_map/abfz,absz->abfs/dot_general | solution.py:240
  814.3 38.4 %psum.7 = f32[]{:T(128)} all-reduce(f32[]{:T(128)S(6)} %mul_shard_map.3), channel_id=1, replica_groups=mesh['grp'=4,'pen'=8] {'grp','pen'}, use_global_device_ids=true, to_apply=%region_1.6 | all-reduce | flops 1 | bytes 8 | tf_op jit(solution)/shard_map/psum | solution.py:252
  869.1 6.2 fusion.282
  916.1 6.8 maximum_bitcast_fusion
  922.9 4.5 maximum_bitcast_fusion.1
  927.5 5.3 maximum_bitcast_fusion.2
  933.8 5.2 maximum_bitcast_fusion.3
  939.1 18.5 %pad_maximum_fusion = f32[32,16,4,2,4,2,256]{6,3,0,5,1,4,2:T(2,128)} fusion(f32[32,16,1,2,4,2,256]{6,3,0,5,1,4,2:T(2,128)} %maximum_bitcast_fusion.3, f32[32,16,1,2,4,2,256]{6,3,0,5,1,4,2:T(2,128)} %maximum_bitcast_fusion.2, f32[32,16,1,2,4,2,256]{6,3,0,5,1,4,2:T(2,128)S(1)} %maximum_bitcast_fusion.1, f32[32,16,1,2,4,2,256]{6,3,0,5,1,4,2:T(2,128)S(1)} %maximum_bitcast_fusion), kind=kLoop, calls=%fused_computation | loop fusion | flops 25165824 | bytes 67108864 | tf_op jit(solution)/shard_map/stack | solution.py:204
  957.5 46.1 %copy.321 = f32[32,16,4,2,4,2,256]{6,5,4,3,2,1,0:T(2,128)} copy(f32[32,16,4,2,4,2,256]{6,3,0,5,1,4,2:T(2,128)} %pad_maximum_fusion) | data formatting | bytes 67108864 | tf_op jit(solution)/shard_map/stack | solution.py:204
  1003.6 39.9 %reshape.1944 = f32[32,16,64,256]{3,2,1,0:T(8,128)} reshape(f32[32,16,4,2,4,2,256]{6,5,4,3,2,1,0:T(2,128)} %copy.321) | data formatting | bytes 67108864 | tf_op jit(solution)/shard_map/reshape | solution.py:204
  1043.6 42.5 %fusion.12 = f32[32,16,64,8]{2,3,1,0:T(8,128)} fusion(f32[32,16,64,8]{2,3,1,0:T(8,128)S(1)} %bitcast.442, f32[32,16,64,256]{3,2,1,0:T(8,128)} %reshape.1944, f32[32,16,64,256]{3,2,1,0:T(8,128)} %fusion.294), kind=kOutput, calls=%fused_computation.21 | convolution fusion | flops 6446383104 | bytes 69206016 | tf_op jit(solution)/shard_map/abfz,absz->abfs/dot_general | solution.py:240
  1086.1 41.7 %fusion.13 = (f32[32,16,64,8]{2,3,1,0:T(8,128)}, f32[32,16,64,8]{2,3,1,0:T(8,128)}) fusion(f32[32,16,64,8]{2,3,1,0:T(8,128)} %get-tuple-element.128, f32[32,16,64,8]{2,3,1,0:T(8,128)S(1)} %bitcast.443, f32[32,16,64,256]{3,2,1,0:T(8,128)} %reshape.1944, f32[32,16,64,256]{3,2,1,0:T(8,128)} %select_add_fusion.1.clone.4), kind=kOutput, calls=%fused_computation.24 | convolution fusion | flops 6450315264 | bytes 71303168 | tf_op jit(solution)/shard_map/abfz,absz->abfs/dot_general | solution.py:237
  1127.9 4.9 multiply_reduce_fusion.2
  (327 shorter events, 248.0 us)
Async XLA Ops:
  10.0 3.7 copy-start.20
  13.3 7.9 copy-start.32
  13.3 7.9 copy-start.34
  13.3 7.8 copy-start.36
  13.3 7.8 copy-start.38
  13.4 7.8 copy-start.40
  13.4 7.8 copy-start.42
  13.5 3.9 copy-start.44
  13.6 3.8 copy-start.90
  17.6 4.9 copy-start.54
  17.6 4.9 copy-start.56
  17.6 4.9 copy-start.58
  17.6 4.9 copy-start.60
  17.6 4.9 copy-start.62
  17.7 4.9 copy-start.64
  361.1 8.6 collective-permute-start
  371.5 9.1 collective-permute-start.1
  451.8 55.0 %all-to-all-start.1 = ((f32[64,4,2176]{2,0,1:T(8,128)}), f32[64,4,2176]{2,0,1:T(8,128)S(1)}, u32[]{:S(2)}, u32[]{:S(2)}) async-start(f32[64,4,2176]{2,0,1:T(8,128)} %copy.297), calls=%async_computation.1 | async-start | bytes 4456448 | tf_op jit(solution)/shard_map/all_to_all | solution.py:153
  695.1 4.3 copy-start.6
  699.9 57.0 %collective-permute-start.2 = (f32[5,32,256]{2,0,1:T(8,128)S(1)}, f32[5,32,256]{2,0,1:T(8,128)S(1)}, u32[]{:S(2)}, u32[]{:S(2)}) collective-permute-start(f32[5,32,256]{2,0,1:T(8,128)S(1)} %slice.369), channel_id=1, source_target_pairs={{8,0},{16,8},{24,16},{0,24},{9,1},{17,9},{25,17},{1,25},{10,2},{18... | collective-permute-start | bytes 491528 | tf_op jit(solution)/shard_map/ppermute | solution.py:18
  757.0 111.8 %collective-permute-start.3 = (f32[70,5,256]{2,0,1:T(8,128)S(1)}, f32[70,5,256]{2,0,1:T(8,128)S(1)}, u32[]{:S(2)}, u32[]{:S(2)}) collective-permute-start(f32[70,5,256]{2,0,1:T(8,128)S(1)} %pad_maximum_fusion.10), channel_id=1, source_target_pairs={{1,0},{2,1},{3,2},{4,3},{5,4},{6,5},{7,6},{0,7},{9,8},{10,9},{11,1... | collective-permute-start | bytes 1075208 | tf_op jit(solution)/shard_map/ppermute | solution.py:18
  906.4 3.8 copy-start.2
  916.0 6.8 copy-start.10
  916.0 6.8 copy-start.11
  916.1 6.8 copy-start.12
  916.1 6.8 copy-start.14
  922.9 4.5 copy-start.8
  922.9 4.5 copy-start.13
  922.9 4.5 copy-start.15
  922.9 4.5 copy-start.17
  927.4 5.3 copy-start.7
  927.4 5.3 copy-start.16
  927.5 5.6 copy-start.18
  927.5 6.4 copy-start.19
  1003.6 39.9 %copy-start.1 = (f32[32,16,8,64]{3,2,1,0:T(8,128)S(1)}, f32[32,16,8,64]{3,2,1,0:T(8,128)}, u32[]{:S(2)}) copy-start(f32[32,16,8,64]{3,2,1,0:T(8,128)} %copy-done) | copy-start | bytes 3145732
  1086.1 41.7 %copy-start.21 = (s32[32,16,64]{2,1,0:T(8,128)S(1)}, s32[32,16,64]{2,1,0:T(8,128)}, u32[]{:S(2)}) copy-start(s32[32,16,64]{2,1,0:T(8,128)} %copy-done.20) | copy-start | bytes 393220
  1086.1 41.7 %copy-start.23 = (s32[32,16,64]{2,1,0:T(8,128)S(1)}, s32[32,16,64]{2,1,0:T(8,128)}, u32[]{:S(2)}) copy-start(s32[32,16,64]{2,1,0:T(8,128)} %copy-done.22) | copy-start | bytes 393220
  1086.1 41.7 %copy-start.25 = (s32[32,16,64]{2,1,0:T(8,128)S(1)}, s32[32,16,64]{2,1,0:T(8,128)}, u32[]{:S(2)}) copy-start(s32[32,16,64]{2,1,0:T(8,128)} %copy-done.24) | copy-start | bytes 393220
  1086.1 41.7 %copy-start.27 = (s32[32,16,64]{2,1,0:T(8,128)S(1)}, s32[32,16,64]{2,1,0:T(8,128)}, u32[]{:S(2)}) copy-start(s32[32,16,64]{2,1,0:T(8,128)} %copy-done.26) | copy-start | bytes 393220
  1086.1 41.7 %copy-start.29 = (s32[32,16,64]{2,1,0:T(8,128)S(1)}, s32[32,16,64]{2,1,0:T(8,128)}, u32[]{:S(2)}) copy-start(s32[32,16,64]{2,1,0:T(8,128)} %copy-done.28) | copy-start | bytes 393220
  1127.8 4.9 copy-start.4
  1127.8 4.9 copy-start.31
  1127.8 4.9 copy-start.83
  1127.8 4.9 copy-start.84
  1127.9 4.9 copy-start.85
  1127.9 4.9 copy-start.86
  1127.9 4.9 copy-start.87
  1127.9 4.9 copy-start.88
  (52 other events, 144.5 us)
where the time goes:
time: 1150 us; the launch traced here: 1140 us
  local copies, waits for them, and re-layouts  445 us (39%)
  matrix products  265 us (23%)
  other arithmetic  200 us (17%)
  blocking collectives  155 us (13%)
  waiting for transfers between devices  60.1 us (5%)
    dot_general x1, matrix products, local(): spread = jnp.einsum('abfs,absz->abfz', pair, weight_z, precision=highest)  141 us
    transpose x17, local copies, waits for them, and re-layouts, place_tiles(): jnp.transpose(shaped[:, :, i, :, j], (0, 2, 1, 3, 4))  86.3 us
    dot_general x2, other arithmetic, local(): jnp.einsum('abxs,abys,abxys->abs', grade_x, weight_y, main, precision=hig...  60.3 us
    reshape x16, local copies, waits for them, and re-layouts, place_tiles(): jnp.transpose(shaped[:, :, i, :, j], (0, 2, 1, 3, 4))  59.5 us
    dot_general x1, other arithmetic, local(): jnp.einsum('abfz,absz->abfs', footing, grade_z, precision=highest)  55.3 us
    all_to_all x1, blocking collectives, spectrum_pen_first(): lax.all_to_all(returning, 'grp', split_axis=0, concat_axis=1, tiled=True)  54 us
    all_to_all x1, waiting for transfers between devices, spectrum_pen_first(): lax.all_to_all(sectioned, 'grp', split_axis=1, concat_axis=0, tiled=True)  50.4 us
    reshape x16, local copies, waits for them, and re-layouts, gather_tiles(): part = part.reshape(tiles_x, 2, tiles_y, 2, KZ)  50 us
  transfers between devices with their start and end apart: 5, of which 3 were waited for; matrix products, arithmetic and copies ran while one was open for 12% of the time, Pallas kernels for 0%

commit v1 on v0

--- a/solution.py
+++ b/solution.py
@@ -10,6 +10,32 @@
 ATOMS = 1048576
 ewald_split = 0.6
 highest = lax.Precision.HIGHEST
+
+
+def _supply_all_face(packet, k_dim, inp):
+    carry_in, k_now = (packet.shape[:k_dim], packet.shape[k_dim + 1 :])
+    return jnp.moveaxis(packet.reshape(*carry_in, inp, -1, *k_now), k_dim, 0)
+
+
+def bars_connect(point, join_dim):
+    wide_out = list(point.shape[1:])
+    wide_out[join_dim] *= point.shape[0]
+    return jnp.moveaxis(point, 0, join_dim).reshape(wide_out)
+
+
+def lift_layers_all(row_data, group_axis, body, chunk):
+    formed, y2 = (lax.axis_size(group_axis), lax.axis_index(group_axis))
+    v_now = _supply_all_face(row_data, body, formed)
+    chunks = [v_now[y2]]
+    idx = 1
+    while idx < formed:
+        inter = v_now[y2 ^ idx]
+        chunks.append(
+            lax.ppermute(inter, axis_name=group_axis, perm=[(k0, k0 ^ idx) for k0 in range(formed)])
+        )
+        idx += 1
+    v_now = jnp.stack(chunks)[y2 ^ jnp.arange(formed)]
+    return bars_connect(v_now, chunk)
 
 
 def shifted(block, axis, distance):
@@ -162,7 +188,7 @@
     scaled = jnp.stack([kernel * real_x, kernel * imag_x], axis=-1).reshape(KX, lines * planes * 2)
     real_b, imag_b = inverse_complex(scaled, cos_x, sin_x, (KX, lines, planes, 2), 3)
     returning = jnp.stack([real_b, imag_b], axis=-1).reshape(KX, lines * planes * 2)
-    rows_home = lax.all_to_all(returning, "grp", split_axis=0, concat_axis=1, tiled=True)
+    rows_home = lift_layers_all(returning, "grp", 0, chunk=1)
     rows_home = jnp.transpose(rows_home.reshape(block_x, KY, planes, 2), (1, 2, 3, 0)).reshape(
         KY, planes * 2 * block_x
     )

time: 1150 us -> 1160 us (level)
  blocking collectives: 155 us -> 110 us
  waiting for transfers between devices: 60.1 us -> 92.6 us
  local copies, waits for them, and re-layouts: 445 us -> 465 us
    all_to_all x1 -> x0, blocking collectives: 54 us -> none  [spectrum_pen_first(): lax.all_to_all(returning, 'grp', split_axis=0, concat_axis=1, tiled=True)]
    ppermute x0 -> x3, waiting for transfers between devices: none -> 32.6 us  [lift_layers_all(): lax.ppermute(inter, axis_name=group_axis, perm=[(k0, k0 ^ idx) for k0 in...]
    dynamic_slice x0 -> x4, local copies, waits for them, and re-layouts: none -> 19.4 us  [the longest x1 11.5 us: lift_layers_all(): chunks = [v_now[y2]]]
    all_to_all x3 -> x0, local copies, waits for them, and re-layouts: 14.1 us -> none  [spectrum_pen_first(): lax.all_to_all(returning, 'grp', split_axis=0, concat_axis=1, tiled=True)]
  transfers between devices with their start and end apart: 5 -> 8, of which waited for: 3 -> 5; matrix products, arithmetic and copies ran while one was open for 12% -> 12% of each run, Pallas kernels for 0% -> 0%
where the time goes in v1:
time: 1160 us; the launch traced here: 1150 us
  local copies, waits for them, and re-layouts  465 us (40%)
  matrix products  265 us (23%)
  other arithmetic  202 us (17%)
  blocking collectives  110 us (9%)
  waiting for transfers between devices  92.6 us (8%)
  starting transfers between devices  13.1 us (1%)
    dot_general x1, matrix products, local(): spread = jnp.einsum('abfs,absz->abfz', pair, weight_z, precision=highest)  141 us
    transpose x17, local copies, waits for them, and re-layouts, place_tiles(): jnp.transpose(shaped[:, :, i, :, j], (0, 2, 1, 3, 4))  86.4 us
    dot_general x2, other arithmetic, local(): jnp.einsum('abxs,abys,abxys->abs', grade_x, weight_y, main, precision=hig...  60.2 us
    reshape x16, local copies, waits for them, and re-layouts, place_tiles(): jnp.transpose(shaped[:, :, i, :, j], (0, 2, 1, 3, 4))  59.6 us
    dot_general x1, other arithmetic, local(): jnp.einsum('abfz,absz->abfs', footing, grade_z, precision=highest)  55.3 us
    all_to_all x1, waiting for transfers between devices, spectrum_pen_first(): lax.all_to_all(sectioned, 'grp', split_axis=1, concat_axis=0, tiled=True)  50.4 us
    reshape x16, local copies, waits for them, and re-layouts, gather_tiles(): part = part.reshape(tiles_x, 2, tiles_y, 2, KZ)  50.1 us
    psum x1, blocking collectives, local(): total = lax.psum(spectral, ('grp', 'pen'))  48.1 us
  transfers between devices with their start and end apart: 8, of which 5 were waited for; matrix products, arithmetic and copies ran while one was open for 12% of the time, Pallas kernels for 0%

profile of v1, /device:TPU:0, one launch (start us, length us, event | category | flops | bytes accessed | tf_op | source)
XLA Modules:
  0.0 1151.9 jit_solution(1173826163659423191)
XLA Ops:
  22.6 140.6 %fusion.15 = f32[32,16,64,256]{3,2,1,0:T(8,128)} fusion(f32[32,16,64]{2,1,0:T(8,128)S(1)} %copy-done.60, s32[32,16,64]{2,1,0:T(8,128)S(1)} %get-tuple-element.188, f32[32,16,64]{2,1,0:T(8,128)S(1)} %copy-done.58, s32[32,16,64]{2,1,0:T(8,128)S(1)} %get-tuple-element.187, f32[32,16,64]{2,1,0:T(8,128)S(1)} %copy-done.54, ...), kind=kOutput, calls=%fused_computation.28 | convolution fusion | flops 6589251584 | bytes 37355520 | tf_op jit(solution)/shard_map/abfs,absz->abfz/dot_general | solution.py:249
  163.3 39.0 %reshape.1914 = f32[32,16,4,2,4,2,256]{6,5,4,3,2,1,0:T(2,128)} reshape(f32[32,16,64,256]{3,2,1,0:T(8,128)} %fusion.15) | data formatting | bytes 67108864 | tf_op jit(solution)/shard_map/reshape | solution.py:210
  202.2 25.3 %slice_bitcast_fusion.15 = (f32[32,2,16,2,256]{4,3,1,2,0:T(2,128)S(1)}, f32[32,2,16,2,256]{4,3,1,2,0:T(2,128)S(1)}, f32[32,2,16,2,256]{4,3,1,2,0:T(2,128)}, f32[...) fusion(f32[32,16,4,2,4,2,256]{6,5,4,3,2,1,0:T(2,128)} %reshape.1914), kind=kLoop, calls=%fused_computation.95 | loop fusion | bytes 67108864 | tf_op jit(solution)/shard_map/transpose | solution.py:214
  241.3 4.1 copy.289
  257.0 4.1 copy.291
  291.8 4.1 reshape.1923
  303.6 4.1 copy.297
  319.0 4.1 copy.299
  348.3 12.9 %pad_add_fusion = f32[70,38,256]{2,0,1:T(8,128)S(1)} fusion(f32[64,32,256]{2,0,1:T(8,128)} %reshape.1930, f32[64,32,256]{2,0,1:T(8,128)} %reshape.1929, f32[64,32,256]{2,0,1:T(8,128)} %reshape.1928, f32[64,32,256]{2,0,1:T(8,128)} %reshape.1927, f32[64,32,256]{2,0,1:T(8,128)} %reshape.1926, f32[64,32,256]{2,0,1:T(8,128)} %reshape.1925, ...), kind=kLoop, calls=%fused_computation.53 | loop fusion | flops 10214400 | bytes 36278272 | tf_op jit(solution)/shard_map/add | solution.py:217
  365.2 4.7 collective-permute-done
  375.9 5.0 collective-permute-done.1
  389.3 7.5 copy.303
  396.8 4.6 all_to_all.40
  401.9 31.4 %all_to_all.54 = f32[32,8,2176]{2,0,1:T(8,128)} all-to-all(f32[32,8,2176]{2,0,1:T(8,128)S(1)} %copy.304), channel_id=1, replica_groups=mesh['grp'=4,'pen'=8] {'pen'}, dimensions={1} | all-to-all | bytes 4456448 | tf_op jit(solution)/shard_map/all_to_all | solution.py:174
  441.8 5.0 copy.309
  446.9 5.1 copy.310
  456.6 50.4 %all-to-all-done.1 = f32[64,4,2176]{2,0,1:T(8,128)S(1)} async-done(((f32[64,4,2176]{2,0,1:T(8,128)}), f32[64,4,2176]{2,0,1:T(8,128)S(1)}, u32[]{:S(2)}, u32[]{:S(2)}) %all-to-all-start.1) | async-done | bytes 2228256 | tf_op jit(solution)/shard_map/all_to_all | solution.py:179
  535.3 4.8 reshape_reshape.6
  540.2 11.5 constant_dynamic-slice_fusion
  565.3 12.1 %collective-permute-done.2 = f32[64,2176]{1,0:T(8,128)} collective-permute-done((f32[64,2176]{1,0:T(8,128)}, f32[64,2176]{1,0:T(8,128)}, u32[]{:S(2)}, u32[]{:S(2)}) %collective-permute-start.2) | collective-permute-done | bytes 557088 | tf_op jit(solution)/shard_map/ppermute | solution.py:34
  577.4 20.5 %collective-permute-done.3 = f32[64,2176]{1,0:T(8,128)S(1)} collective-permute-done((f32[64,2176]{1,0:T(8,128)}, f32[64,2176]{1,0:T(8,128)S(1)}, u32[]{:S(2)}, u32[]{:S(2)}) %collective-permute-start.3) | collective-permute-done | bytes 557088 | tf_op jit(solution)/shard_map/ppermute | solution.py:34
  602.1 4.7 copy.328
  606.8 7.0 copy.388
  613.9 6.1 copy.329
  620.0 4.6 fusion.36
  628.2 5.0 copy.333
  633.3 5.0 all_to_all.48
  638.3 30.4 %all_to_all.55 = f32[8,32,2176]{2,1,0:T(8,128)S(1)} all-to-all(f32[8,32,2176]{2,1,0:T(8,128)S(1)} %all_to_all.48), channel_id=1, replica_groups=mesh['grp'=4,'pen'=8] {'pen'}, dimensions={0} | all-to-all | bytes 4456448 | tf_op jit(solution)/shard_map/all_to_all | solution.py:197
  670.0 4.1 reshape.1933
  674.1 8.8 fusion.281
  682.9 5.8 copy.395
  688.7 5.3 fusion.141
  694.0 4.4 copy.394
  698.4 4.2 fusion.143
  704.8 55.4 %select_add_fusion.1.clone.4 = f32[32,16,64,256]{3,2,1,0:T(8,128)} fusion(f32[32,16,64]{2,1,0:T(8,128)S(1)} %copy-done.61, s32[32,16,64]{2,1,0:T(8,128)S(1)} %copy-done.43, f32[32,16,64]{2,1,0:T(8,128)S(1)} %copy-done.59, s32[32,16,64]{2,1,0:T(8,128)S(1)} %copy-done.41, f32[32,16,64]{2,1,0:T(8,128)S(1)} %copy-done.55, ...), kind=kLoop, calls=%fused_computation.14.clone.clone.clone.clone.1 | loop fusion | flops 142606336 | bytes 35127296 | tf_op jit(solution)/shard_map/abxs,abys,abxys->abs/dot_general | solution.py:269
  761.6 55.3 %fusion.295 = f32[32,16,64,256]{3,2,1,0:T(8,128)} fusion(f32[32,16,64]{2,1,0:T(8,128)S(1)} %copy-done.53, f32[32,16,64]{2,1,0:T(8,128)S(1)} %copy-done.51, f32[32,16,64]{2,1,0:T(8,128)S(1)} %copy-done.50, f32[32,16,64]{2,1,0:T(8,128)S(1)} %copy-done.52, f32[32,16,64]{2,1,0:T(8,128)S(1)} %copy-done.49, f32[32,16,64]{2,1,0:T(8,128)S(1)} %copy-done.48, ...), kind=kLoop, calls=%fused_computation.3.clone.clone.clone.1 | loop fusion | flops 142606336 | bytes 35127296 | tf_op jit(solution)/shard_map/abfz,absz->abfs/dot_general | solution.py:266
  817.6 48.1 %psum.7 = f32[]{:T(128)} all-reduce(f32[]{:T(128)S(6)} %mul_shard_map.3), channel_id=1, replica_groups=mesh['grp'=4,'pen'=8] {'grp','pen'}, use_global_device_ids=true, to_apply=%region_1.6 | all-reduce | flops 1 | bytes 8 | tf_op jit(solution)/shard_map/psum | solution.py:278
  882.1 6.2 fusion.283
  929.1 6.8 maximum_bitcast_fusion
  936.0 4.5 maximum_bitcast_fusion.1
  940.6 5.3 maximum_bitcast_fusion.2
  946.9 5.2 maximum_bitcast_fusion.3
  952.1 18.5 %pad_maximum_fusion = f32[32,16,4,2,4,2,256]{6,3,0,5,1,4,2:T(2,128)} fusion(f32[32,16,1,2,4,2,256]{6,3,0,5,1,4,2:T(2,128)} %maximum_bitcast_fusion.3, f32[32,16,1,2,4,2,256]{6,3,0,5,1,4,2:T(2,128)} %maximum_bitcast_fusion.2, f32[32,16,1,2,4,2,256]{6,3,0,5,1,4,2:T(2,128)S(1)} %maximum_bitcast_fusion.1, f32[32,16,1,2,4,2,256]{6,3,0,5,1,4,2:T(2,128)S(1)} %maximum_bitcast_fusion), kind=kLoop, calls=%fused_computation.1 | loop fusion | flops 25165824 | bytes 67108864 | tf_op jit(solution)/shard_map/stack | solution.py:230
  970.6 46.1 %copy.337 = f32[32,16,4,2,4,2,256]{6,5,4,3,2,1,0:T(2,128)} copy(f32[32,16,4,2,4,2,256]{6,3,0,5,1,4,2:T(2,128)} %pad_maximum_fusion) | data formatting | bytes 67108864 | tf_op jit(solution)/shard_map/stack | solution.py:230
  1016.7 39.9 %reshape.1950 = f32[32,16,64,256]{3,2,1,0:T(8,128)} reshape(f32[32,16,4,2,4,2,256]{6,5,4,3,2,1,0:T(2,128)} %copy.337) | data formatting | bytes 67108864 | tf_op jit(solution)/shard_map/reshape | solution.py:230
  1056.7 42.5 %fusion.12 = f32[32,16,64,8]{2,3,1,0:T(8,128)} fusion(f32[32,16,64,8]{2,3,1,0:T(8,128)S(1)} %bitcast.450, f32[32,16,64,256]{3,2,1,0:T(8,128)} %reshape.1950, f32[32,16,64,256]{3,2,1,0:T(8,128)} %fusion.295), kind=kOutput, calls=%fused_computation.22 | convolution fusion | flops 6446383104 | bytes 69206016 | tf_op jit(solution)/shard_map/abfz,absz->abfs/dot_general | solution.py:266
  1099.2 41.7 %fusion.13 = (f32[32,16,64,8]{2,3,1,0:T(8,128)}, f32[32,16,64,8]{2,3,1,0:T(8,128)}) fusion(f32[32,16,64,8]{2,3,1,0:T(8,128)} %get-tuple-element.132, f32[32,16,64,8]{2,3,1,0:T(8,128)S(1)} %bitcast.451, f32[32,16,64,256]{3,2,1,0:T(8,128)} %reshape.1950, f32[32,16,64,256]{3,2,1,0:T(8,128)} %select_add_fusion.1.clone.4), kind=kOutput, calls=%fused_computation.25 | convolution fusion | flops 6450315264 | bytes 71303168 | tf_op jit(solution)/shard_map/abfz,absz->abfs/dot_general | solution.py:263
  1141.0 4.9 multiply_reduce_fusion.2
  (342 shorter events, 270.2 us)
Async XLA Ops:
  13.4 7.8 copy-start.32
  13.4 7.8 copy-start.34
  13.4 7.8 copy-start.36
  13.4 7.8 copy-start.38
  13.4 7.8 copy-start.40
  13.4 7.8 copy-start.42
  13.6 3.9 copy-start.44
  17.7 4.9 copy-start.54
  17.7 4.9 copy-start.56
  17.7 4.9 copy-start.58
  17.7 4.9 copy-start.60
  17.7 4.9 copy-start.62
  17.7 4.9 copy-start.64
  361.3 8.6 collective-permute-start
  371.6 9.2 collective-permute-start.1
  451.9 55.0 %all-to-all-start.1 = ((f32[64,4,2176]{2,0,1:T(8,128)}), f32[64,4,2176]{2,0,1:T(8,128)S(1)}, u32[]{:S(2)}, u32[]{:S(2)}) async-start(f32[64,4,2176]{2,0,1:T(8,128)} %copy.310), calls=%async_computation.1 | async-start | bytes 4456448 | tf_op jit(solution)/shard_map/all_to_all | solution.py:179
  555.2 22.2 %collective-permute-start.2 = (f32[64,2176]{1,0:T(8,128)}, f32[64,2176]{1,0:T(8,128)}, u32[]{:S(2)}, u32[]{:S(2)}) collective-permute-start(f32[64,2176]{1,0:T(8,128)} %bitcast.482), channel_id=1, source_target_pairs={{0,8},{8,0},{16,24},{24,16},{1,9},{9,1},{17,25},{25,17},{2,10},{10... | collective-permute-start | bytes 1671176 | tf_op jit(solution)/shard_map/ppermute | solution.py:34
  557.4 40.5 %collective-permute-start.3 = (f32[64,2176]{1,0:T(8,128)}, f32[64,2176]{1,0:T(8,128)S(1)}, u32[]{:S(2)}, u32[]{:S(2)}) collective-permute-start(f32[64,2176]{1,0:T(8,128)} %bitcast.483), channel_id=1, source_target_pairs={{0,16},{8,24},{16,0},{24,8},{1,17},{9,25},{17,1},{25,9},{2,18},{10... | collective-permute-start | bytes 1671176 | tf_op jit(solution)/shard_map/ppermute | solution.py:34
  561.6 36.3 %collective-permute-start.4 = (f32[64,2176]{1,0:T(8,128)}, f32[64,2176]{1,0:T(8,128)S(1)}, u32[]{:S(2)}, u32[]{:S(2)}) collective-permute-start(f32[64,2176]{1,0:T(8,128)} %bitcast.87), channel_id=1, source_target_pairs={{0,24},{8,16},{16,8},{24,0},{1,25},{9,17},{17,9},{25,1},{2,26},{10... | collective-permute-start | bytes 1671176 | tf_op jit(solution)/shard_map/ppermute | solution.py:34
  698.4 4.3 copy-start.6
  703.2 57.1 %collective-permute-start.5 = (f32[5,32,256]{2,0,1:T(8,128)S(1)}, f32[5,32,256]{2,0,1:T(8,128)S(1)}, u32[]{:S(2)}, u32[]{:S(2)}) collective-permute-start(f32[5,32,256]{2,0,1:T(8,128)S(1)} %slice.371), channel_id=1, source_target_pairs={{8,0},{16,8},{24,16},{0,24},{9,1},{17,9},{25,17},{1,25},{10,2},{18... | collective-permute-start | bytes 491528 | tf_op jit(solution)/shard_map/ppermute | solution.py:44
  760.3 121.5 %collective-permute-start.6 = (f32[70,5,256]{2,0,1:T(8,128)S(1)}, f32[70,5,256]{2,0,1:T(8,128)S(1)}, u32[]{:S(2)}, u32[]{:S(2)}) collective-permute-start(f32[70,5,256]{2,0,1:T(8,128)S(1)} %pad_maximum_fusion.11), channel_id=1, source_target_pairs={{1,0},{2,1},{3,2},{4,3},{5,4},{6,5},{7,6},{0,7},{9,8},{10,9},{11,1... | collective-permute-start | bytes 1075208 | tf_op jit(solution)/shard_map/ppermute | solution.py:44
  929.1 6.8 copy-start.10
  929.1 6.8 copy-start.11
  929.1 6.8 copy-start.12
  929.1 6.8 copy-start.14
  936.0 4.5 copy-start.8
  936.0 4.5 copy-start.13
  936.0 4.5 copy-start.15
  936.0 4.5 copy-start.17
  940.5 5.3 copy-start.7
  940.5 5.3 copy-start.16
  940.5 5.6 copy-start.18
  940.5 6.4 copy-start.19
  1016.7 39.9 %copy-start.1 = (f32[32,16,8,64]{3,2,1,0:T(8,128)S(1)}, f32[32,16,8,64]{3,2,1,0:T(8,128)}, u32[]{:S(2)}) copy-start(f32[32,16,8,64]{3,2,1,0:T(8,128)} %copy-done) | copy-start | bytes 3145732
  1099.2 41.7 %copy-start.21 = (s32[32,16,64]{2,1,0:T(8,128)S(1)}, s32[32,16,64]{2,1,0:T(8,128)}, u32[]{:S(2)}) copy-start(s32[32,16,64]{2,1,0:T(8,128)} %copy-done.20) | copy-start | bytes 393220
  1099.2 41.7 %copy-start.23 = (s32[32,16,64]{2,1,0:T(8,128)S(1)}, s32[32,16,64]{2,1,0:T(8,128)}, u32[]{:S(2)}) copy-start(s32[32,16,64]{2,1,0:T(8,128)} %copy-done.22) | copy-start | bytes 393220
  1099.2 41.7 %copy-start.25 = (s32[32,16,64]{2,1,0:T(8,128)S(1)}, s32[32,16,64]{2,1,0:T(8,128)}, u32[]{:S(2)}) copy-start(s32[32,16,64]{2,1,0:T(8,128)} %copy-done.24) | copy-start | bytes 393220
  1099.2 41.7 %copy-start.27 = (s32[32,16,64]{2,1,0:T(8,128)S(1)}, s32[32,16,64]{2,1,0:T(8,128)}, u32[]{:S(2)}) copy-start(s32[32,16,64]{2,1,0:T(8,128)} %copy-done.26) | copy-start | bytes 393220
  1099.2 41.7 %copy-start.29 = (s32[32,16,64]{2,1,0:T(8,128)S(1)}, s32[32,16,64]{2,1,0:T(8,128)}, u32[]{:S(2)}) copy-start(s32[32,16,64]{2,1,0:T(8,128)} %copy-done.28) | copy-start | bytes 393220
  1140.9 4.9 copy-start.4
  1140.9 4.9 copy-start.31
  1140.9 4.9 copy-start.83
  1141.0 4.9 copy-start.84
  1141.0 4.9 copy-start.85
  1141.0 4.9 copy-start.86
  1141.0 4.9 copy-start.87
  1141.0 4.9 copy-start.88
  (56 other events, 157.0 us)
